TPU v7x, 32 devices: a whole 2x2x4 slice. The times are simulated.
32 devices in a mesh: parts: 2 (over y), patch: 4 (over z), sub: 2 (over x), lvl: 2 (over core).
Axes of the slice: x: 2, y: 2, z: 4, core: 2. Of those that a mesh axis runs over, the one named last changes fastest.
Arguments:
- node_states: float32 [8192, 512], P(('parts', 'patch', 'lvl')), parts along dimension 0, may hold values from -6 to 6
- coarse_states: float32 [1024, 512], P(('parts', 'patch', 'lvl')), parts along dimension 0, may hold values from -6 to 6
- children: int32 [512, 7], P(('patch', 'lvl')), may hold values from 0 to 511
- down_sources: int32 [4096, 3], P(('patch', 'lvl')), may hold values from 0 to 63
- bottom_links: int32 [4096, 6], P(('patch', 'lvl')), may hold values from 0 to 767, as said below
- coarse_links: int32 [512, 6], P(('patch', 'lvl')), may hold values from 0 to 511
- upward_sender: float32 [512, 512], P(None, 'sub'), may hold values from -0.25 to 0.25
- upward_receiver: float32 [512, 512], P(None, 'sub'), may hold values from -0.25 to 0.25
- upward_bias: float32 [512], P('sub'), may hold values from -4 to 4
- upward_output: float32 [512, 512], P('sub'), may hold values from -0.25 to 0.25
- upward_gain: float32 [512], replicated, may hold values from 0.1 to 1.9
- coarse_sender: float32 [512, 512], P(None, 'sub'), may hold values from -0.25 to 0.25
- coarse_receiver: float32 [512, 512], P(None, 'sub'), may hold values from -0.25 to 0.25
- coarse_bias: float32 [512], P('sub'), may hold values from -4 to 4
- coarse_output: float32 [512, 512], P('sub'), may hold values from -0.25 to 0.25
- coarse_gain: float32 [512], replicated, may hold values from 0.1 to 1.9
- downward_sender: float32 [512, 512], P(None, 'sub'), may hold values from -0.25 to 0.25
- downward_receiver: float32 [512, 512], P(None, 'sub'), may hold values from -0.25 to 0.25
- downward_bias: float32 [512], P('sub'), may hold values from -4 to 4
- downward_output: float32 [512, 512], P('sub'), may hold values from -0.25 to 0.25
- downward_gain: float32 [512], replicated, may hold values from 0.1 to 1.9
- bottom_sender: float32 [512, 512], P(None, 'sub'), may hold values from -0.25 to 0.25
- bottom_receiver: float32 [512, 512], P(None, 'sub'), may hold values from -0.25 to 0.25
- bottom_bias: float32 [512], P('sub'), may hold values from -4 to 4
- bottom_output: float32 [512, 512], P('sub'), may hold values from -0.25 to 0.25
- bottom_gain: float32 [512], replicated, may hold values from 0.1 to 1.9
Outputs:
- new_nodes: float32 [8192, 512], P(('parts', 'patch', 'lvl')), parts along dimension 0
- new_coarse: float32 [1024, 512], P(('parts', 'patch', 'lvl')), parts along dimension 0
There are 2 independent parts, one for each index of `parts`. A program takes and returns all parts, laid end to end along the dimension named above; an argument that names none is the same for every part. Nothing has to cross between parts.
Inputs may be any that keep to these rules, and one draw needn't show every extreme that they name: bottom_links[n, k] - 128 differs from n's row within its block by at most 128.
All inputs are finite; a program needn't handle non-finite values.
Results may differ from a plain program's by a relative error of at most 0.00011.
Values sent between devices are 32-bit elements; how exact they have to be, the bound alone decides.
A program may use at most 64 MiB of HBM per device.

v0:
```python
import jax
import jax.numpy as jnp
from jax import lax
from jax.sharding import PartitionSpec as P

epsilon = 1e-05
highest = lax.Precision.HIGHEST


def extended(cells, sides, width):
    for axis, dim in sides:
        count = lax.axis_size(axis)
        head = lax.slice_in_dim(cells, 0, width, axis=dim)
        tail = lax.slice_in_dim(cells, cells.shape[dim] - width, cells.shape[dim], axis=dim)
        cells = jnp.concatenate(
            [
                lax.ppermute(tail, axis, [(i, (i + 1) % count) for i in range(count)]),
                cells,
                lax.ppermute(head, axis, [((i + 1) % count, i) for i in range(count)]),
            ],
            axis=dim,
        )
    return cells


def project(states, weights):
    return jnp.dot(states, weights, precision=highest, preferred_element_type=jnp.float32)


def layer_norm(values):
    center = values - jnp.mean(values, axis=-1, keepdims=True)
    spread = jnp.mean(center * center, axis=-1, keepdims=True)
    return center * lax.rsqrt(spread + epsilon)


def hidden_total(picked, receiver_rows):
    return jnp.sum(jax.nn.silu(picked + receiver_rows[:, None, :]), axis=1)


def finish(receivers, hidden, output_weights, gain_vector):
    partial_value = project(hidden, output_weights)
    summed = lax.psum(partial_value, "sub")
    return receivers + gain_vector * layer_norm(summed)


def pick_rows(source_rows, wanted):
    inside = (wanted >= 0) & (wanted < source_rows.shape[0])
    picked = jnp.take(source_rows, jnp.clip(wanted, 0, source_rows.shape[0] - 1), axis=0)
    return jnp.where(inside[:, None], picked, 0.0)


def body(
    node_states,
    coarse_states,
    children,
    down_sources,
    bottom_links,
    coarse_links,
    upward_sender,
    upward_receiver,
    upward_bias,
    upward_output,
    upward_gain,
    coarse_sender,
    coarse_receiver,
    coarse_bias,
    coarse_output,
    coarse_gain,
    downward_sender,
    downward_receiver,
    downward_bias,
    downward_output,
    downward_gain,
    bottom_sender,
    bottom_receiver,
    bottom_bias,
    bottom_output,
    bottom_gain,
):
    sender_rows = project(node_states, upward_sender)
    receiver_rows = project(coarse_states, upward_receiver) + upward_bias
    picked = jnp.take(sender_rows, children, axis=0)
    coarse_up = finish(
        coarse_states, hidden_total(picked, receiver_rows), upward_output, upward_gain
    )
    receiver_rows = project(coarse_up, coarse_receiver) + coarse_bias
    flat_links = coarse_links.reshape(-1)
    own_projection = project(coarse_up, coarse_sender)
    gathered = pick_rows(
        lax.all_gather(own_projection, ("patch", "lvl"), axis=0, tiled=True), flat_links
    )
    picked = gathered.reshape(coarse_links.shape[0], coarse_links.shape[1], receiver_rows.shape[1])
    new_coarse = finish(coarse_up, hidden_total(picked, receiver_rows), coarse_output, coarse_gain)
    sender_rows = project(new_coarse, downward_sender)
    receiver_rows = project(node_states, downward_receiver) + downward_bias
    picked = jnp.take(sender_rows, down_sources, axis=0)
    nodes_down = finish(
        node_states, hidden_total(picked, receiver_rows), downward_output, downward_gain
    )
    rim_rows = node_states.shape[0] // 4
    receiver_rows = project(nodes_down, bottom_receiver) + bottom_bias
    own_projection = project(nodes_down, bottom_sender)
    sender_rows = extended(own_projection, ((("patch", "lvl"), 0),), rim_rows)
    picked = jnp.take(sender_rows, bottom_links, axis=0)
    new_nodes = finish(nodes_down, hidden_total(picked, receiver_rows), bottom_output, bottom_gain)
    return (new_nodes, new_coarse)


def solution(mesh):
    in_specs = (
        P(("parts", "patch", "lvl"), None),
        P(("parts", "patch", "lvl"), None),
        P(("patch", "lvl"), None),
        P(("patch", "lvl"), None),
        P(("patch", "lvl"), None),
        P(("patch", "lvl"), None),
        P(None, "sub"),
        P(None, "sub"),
        P("sub"),
        P("sub", None),
        P(),
        P(None, "sub"),
        P(None, "sub"),
        P("sub"),
        P("sub", None),
        P(),
        P(None, "sub"),
        P(None, "sub"),
        P("sub"),
        P("sub", None),
        P(),
        P(None, "sub"),
        P(None, "sub"),
        P("sub"),
        P("sub", None),
        P(),
    )
    out_specs = (P(("parts", "patch", "lvl"), None), P(("parts", "patch", "lvl"), None))
    return jax.shard_map(body, mesh=mesh, in_specs=in_specs, out_specs=out_specs, check_vma=False)
```

profile of v0, /device:TPU:0, one launch (start us, length us, event | category | flops | bytes accessed | tf_op | source)
XLA Modules:
  0.0 235.3 jit_solution(15321210769861987477)
XLA Ops:
  7.2 0.0 all-reduce.5.cloned.1.call-start
  7.2 0.7 compare_select_fusion.3
  8.0 0.7 compare_and_fusion.4
  8.7 0.1 copy.35
  8.8 0.1 reshape.129
  8.9 2.3 fusion.3
  11.3 1.7 gather_fusion
  13.1 0.1 reshape.128
  13.1 0.1 copy.34
  13.3 0.4 convolution_add_fusion.3
  13.7 0.3 multiply_reduce_fusion.4
  14.0 2.1 fusion.4
  16.2 0.0 all-reduce.7.cloned.1.call-start
  16.3 0.1 copy.38
  16.4 0.1 min.12
  16.6 2.0 convolution_add_fusion.1
  18.6 0.1 copy.36
  18.7 0.1 copy.37
  18.9 21.8 %all-reduce.5.cloned.1.call-done = f32[64,512]{1,0:T(8,128)} async-done(((f32[64,512]{1,0:T(8,128)}), f32[64,512]{1,0:T(8,128)}) %all-reduce.5.cloned.1.call-update) | async-done | bytes 131088 | tf_op jit(solution)/shard_map/psum | solution.py:42
  40.6 1.0 reduce_sum.109
  41.6 1.1 multiply_reduce_fusion.6
  42.8 1.0 multiply_add_fusion.3
  43.8 0.4 fusion.5
  44.2 14.7 %all_gather.3 = f32[512,256]{1,0:T(8,128)S(1)} all-gather(f32[64,256]{1,0:T(8,128)S(1)} %fusion.5), channel_id=1, replica_groups=mesh['parts'=2,'patch'=4,'sub'=2,'lvl'=2] {'patch','lvl'}, dimensions={0}, use_global_device_ids=true | all-gather | bytes 589824 | tf_op jit(solution)/shard_map/all_gather | solution.py:90
  58.9 1.7 gather_fusion.1
  60.5 0.1 gather.20
  60.6 1.5 convolution_add_fusion.2
  62.1 0.5 multiply_reduce_fusion.3
  62.6 2.1 fusion.6
  64.8 0.0 all-reduce.9.cloned.1.call-start
  64.8 0.1 copy.39
  65.0 0.2 reshape.145
  65.2 0.2 copy.33
  65.4 21.2 %all-reduce.7.cloned.1.call-done = f32[64,512]{1,0:T(8,128)} async-done(((f32[64,512]{1,0:T(8,128)}), f32[64,512]{1,0:T(8,128)}) %all-reduce.7.cloned.1.call-update) | async-done | bytes 131088 | tf_op jit(solution)/shard_map/psum | solution.py:42
  86.6 1.0 reduce_sum.112
  87.7 1.1 multiply_reduce_fusion.5
  88.8 1.0 multiply_add_fusion.2
  89.8 0.4 fusion.7
  90.2 4.7 %gather_fusion.2 = f32[1536,256]{1,0:T(8,128)} fusion(f32[64,256]{1,0:T(8,128)S(1)} %fusion.7, s32[2048]{0:T(1024)S(1)} %pad_clamp_fusion), kind=kCustom, calls=%fused_computation.2 | custom fusion | bytes 3151872 | tf_op jit(solution)/shard_map/jit(_take)/gather | solution.py:96
  94.9 3.6 %reshape.144 = f32[512,3,256]{2,1,0:T(4,128)} reshape(f32[1536,256]{1,0:T(8,128)} %gather_fusion.2) | data formatting | bytes 3145728 | tf_op jit(solution)/shard_map/jit(_take)/gather | solution.py:96
  98.5 4.4 %fusion = f32[512,256]{1,0:T(8,128)S(1)} fusion(f32[512,3,256]{2,1,0:T(4,128)} %reshape.144, f32[512,256]{1,0:T(8,128)S(1)} %convolution_add_fusion.1, pred[512,3]{1,0:T(8,128)(4,1)S(1)} %copy.33), kind=kLoop, calls=%fused_computation.6 | loop fusion | flops 2621440 | bytes 2622976 | tf_op jit(solution)/shard_map/reduce_sum | solution.py:37
  103.0 2.0 fusion.8
  105.0 0.2 all-reduce.11.cloned.1.call-start
  105.2 0.1 copy.41
  105.4 0.2 reshape.153
  105.6 0.2 copy.40
  105.8 39.4 %all-reduce.9.cloned.1.call-done = f32[512,512]{1,0:T(8,128)} async-done(((f32[512,512]{1,0:T(8,128)}), f32[512,512]{1,0:T(8,128)}) %all-reduce.9.cloned.1.call-update) | async-done | bytes 1048592 | tf_op jit(solution)/shard_map/psum | solution.py:42
  145.2 1.4 reduce_sum.115
  146.6 1.5 multiply_reduce_fusion.2
  148.1 1.5 multiply_add_fusion.1
  149.6 1.0 fusion.9
  150.7 0.1 collective-permute-start
  150.7 3.5 %collective-permute-start.1 = (f32[128,256]{1,0:T(8,128)S(1)}, f32[128,256]{1,0:T(8,128)S(1)}, u32[]{:S(2)}, u32[]{:S(2)}) collective-permute-start(f32[128,256]{1,0:T(8,128)S(1)} %get-tuple-element.3), channel_id=1, source_target_pairs={{1,0},{4,1},{5,4},{8,5},{9,8},{12,9},{13,12},{0,13},{3,2},{6,3},{7... | collective-permute-start | bytes 393224 | tf_op jit(solution)/shard_map/ppermute | solution.py:19
  154.3 1.0 convolution_add_fusion
  155.3 1.7 collective-permute-done
  157.0 0.1 pad_maximum_fusion
  157.1 12.3 %gather_fusion.3 = f32[3072,256]{1,0:T(8,128)} fusion(f32[768,256]{1,0:T(8,128)S(1)} %pad_maximum_fusion, s32[3072]{0:T(1024)S(1)} %broadcast_clamp_fusion), kind=kCustom, calls=%fused_computation.3 | custom fusion | bytes 6303744 | tf_op jit(solution)/shard_map/jit(_take)/gather | solution.py:104
  169.4 4.5 %reshape.152 = f32[512,6,256]{2,1,0:T(8,128)} reshape(f32[3072,256]{1,0:T(8,128)} %gather_fusion.3) | data formatting | bytes 6291456 | tf_op jit(solution)/shard_map/jit(_take)/gather | solution.py:104
  173.9 7.1 %multiply_reduce_fusion = f32[512,256]{1,0:T(8,128)S(1)} fusion(f32[512,6,256]{2,1,0:T(8,128)} %reshape.152, f32[512,256]{1,0:T(8,128)S(1)} %convolution_add_fusion, pred[512,6]{1,0:T(8,128)(4,1)S(1)} %copy.40), kind=kLoop, calls=%fused_computation.4 | loop fusion | flops 5373952 | bytes 4197376 | tf_op jit(solution)/shard_map/reduce_sum | solution.py:37
  181.1 2.0 fusion.10
  183.1 40.4 %all-reduce.11.cloned.1.call-done = f32[512,512]{1,0:T(8,128)} async-done(((f32[512,512]{1,0:T(8,128)}), f32[512,512]{1,0:T(8,128)}) %all-reduce.11.cloned.1.call-update) | async-done | bytes 1048592 | tf_op jit(solution)/shard_map/psum | solution.py:42
  223.5 1.4 reduce_sum.118
  224.9 1.5 multiply_reduce_fusion.1
  226.4 2.4 %multiply_add_fusion = f32[512,512]{1,0:T(8,128)} fusion(f32[512,512]{1,0:T(8,128)S(1)} %multiply_add_fusion.1, f32[512,512]{1,0:T(8,128)} %all-reduce.11.cloned.1.call-done, f32[512]{0:T(512)S(1)} %add_rsqrt_fusion, f32[512]{0:T(512)S(1)} %broadcast_multiply_fusion, f32[512]{0:T(512)S(1)} %copy-done.16), kind=kLoop, calls=%fused_computation.11 | loop fusion | flops 1048576 | bytes 3151872 | tf_op jit(solution)/shard_map/add | solution.py:43
  (67 shorter events, 0.3 us)
Async XLA Ops:
  7.2 95.8 %copy-start = (f32[256,512]{1,0:T(8,128)S(1)}, f32[256,512]{1,0:T(8,128)}, u32[]{:S(2)}) copy-start(f32[256,512]{1,0:T(8,128)} %param.45) | copy-start | bytes 1572868
  7.2 33.4 %all-reduce.5.cloned.1.call-start = ((), (), s32[]{:S(2)}) async-start(), calls=%async_computation | async-start | bytes 262144 | tf_op jit(solution)/shard_map/psum | solution.py:42
  11.3 2.0 copy-start.2
  11.3 2.0 copy-start.5
  11.3 2.0 copy-start.17
  11.3 4.9 %copy-start.12 = (s32[64,6]{0,1:T(8,128)S(1)}, s32[64,6]{0,1:T(8,128)}, u32[]{:S(2)}) copy-start(s32[64,6]{0,1:T(8,128)} %param.31) | copy-start | bytes 4612
  11.3 5.2 %copy-start.11 = (s32[512,3]{0,1:T(4,128)S(1)}, s32[512,3]{0,1:T(4,128)}, u32[]{:S(2)}) copy-start(s32[512,3]{0,1:T(4,128)} %param.29) | copy-start | bytes 18436
  11.3 5.2 %copy-start.1 = (f32[512,512]{1,0:T(8,128)S(1)}, f32[512,512]{1,0:T(8,128)}, u32[]{:S(2)}) copy-start(f32[512,512]{1,0:T(8,128)} %param.26) | copy-start | bytes 3145732
  11.3 5.2 %copy-start.18 = (f32[256]{0:T(256)S(1)}, f32[256]{0:T(256)}, u32[]{:S(2)}) copy-start(f32[256]{0:T(256)} %param.44) | copy-start | bytes 3076
  13.1 29.7 %copy-start.13 = (f32[512]{0:T(512)S(1)}, f32[512]{0:T(512)}, u32[]{:S(2)}) copy-start(f32[512]{0:T(512)} %param.36) | copy-start | bytes 6148
  13.7 30.1 %copy-start.3 = (f32[512,256]{1,0:T(8,128)S(1)}, f32[512,256]{1,0:T(8,128)}, u32[]{:S(2)}) copy-start(f32[512,256]{1,0:T(8,128)} %param.37) | copy-start | bytes 1572868
  16.2 70.4 %all-reduce.7.cloned.1.call-start = ((), (), s32[]{:S(2)}) async-start(), calls=%async_computation.1 | async-start | bytes 262144 | tf_op jit(solution)/shard_map/psum | solution.py:42
  41.6 19.0 %copy-start.19 = (f32[256]{0:T(256)S(1)}, f32[256]{0:T(256)}, u32[]{:S(2)}) copy-start(f32[256]{0:T(256)} %param.39) | copy-start | bytes 3076
  58.9 29.9 %copy-start.14 = (f32[512]{0:T(512)S(1)}, f32[512]{0:T(512)}, u32[]{:S(2)}) copy-start(f32[512]{0:T(512)} %param.41) | copy-start | bytes 6148
  60.6 29.2 %copy-start.4 = (f32[512,256]{1,0:T(8,128)S(1)}, f32[512,256]{1,0:T(8,128)}, u32[]{:S(2)}) copy-start(f32[512,256]{1,0:T(8,128)} %param.42) | copy-start | bytes 1572868
  64.8 80.5 %all-reduce.9.cloned.1.call-start = ((), (), s32[]{:S(2)}) async-start(), calls=%async_computation.2 | async-start | bytes 2097152 | tf_op jit(solution)/shard_map/psum | solution.py:42
  89.8 5.1 %copy-start.6 = (f32[64,512]{1,0:T(8,128)}, f32[64,512]{1,0:T(8,128)S(1)}, u32[]{:S(2)}) copy-start(f32[64,512]{1,0:T(8,128)S(1)} %multiply_add_fusion.2) | copy-start | bytes 393220
  98.5 6.7 %copy-start.10 = (s32[512,6]{0,1:T(8,128)S(1)}, s32[512,6]{0,1:T(8,128)}, u32[]{:S(2)}) copy-start(s32[512,6]{0,1:T(8,128)} %param.30) | copy-start | bytes 36868
  102.9 45.2 %copy-start.15 = (f32[512]{0:T(512)S(1)}, f32[512]{0:T(512)}, u32[]{:S(2)}) copy-start(f32[512]{0:T(512)} %param.46) | copy-start | bytes 6148
  105.0 44.7 %copy-start.7 = (f32[512,256]{1,0:T(8,128)S(1)}, f32[512,256]{1,0:T(8,128)}, u32[]{:S(2)}) copy-start(f32[512,256]{1,0:T(8,128)} %param.47) | copy-start | bytes 1572868
  105.0 118.5 %all-reduce.11.cloned.1.call-start = ((), (), s32[]{:S(2)}) async-start(), calls=%async_computation.3 | async-start | bytes 2097152 | tf_op jit(solution)/shard_map/psum | solution.py:42
  148.1 6.2 %copy-start.8 = (f32[512,256]{1,0:T(8,128)S(1)}, f32[512,256]{1,0:T(8,128)}, u32[]{:S(2)}) copy-start(f32[512,256]{1,0:T(8,128)} %param.48) | copy-start | bytes 1572868
  148.1 6.2 %copy-start.20 = (f32[256]{0:T(256)S(1)}, f32[256]{0:T(256)}, u32[]{:S(2)}) copy-start(f32[256]{0:T(256)} %param.49) | copy-start | bytes 3076
  150.7 6.3 %collective-permute-start = (f32[128,256]{1,0:T(8,128)S(1)}, f32[128,256]{1,0:T(8,128)S(1)}, u32[]{:S(2)}, u32[]{:S(2)}) collective-permute-start(f32[128,256]{1,0:T(8,128)S(1)} %get-tuple-element.2), channel_id=1, source_target_pairs={{0,1},{1,4},{4,5},{5,8},{8,9},{9,12},{12,13},{13,0},{2,3},{3,6},{6... | collective-permute-start | bytes 393224 | tf_op jit(solution)/shard_map/ppermute | solution.py:17
  150.7 6.3 %collective-permute-start.1 = (f32[128,256]{1,0:T(8,128)S(1)}, f32[128,256]{1,0:T(8,128)S(1)}, u32[]{:S(2)}, u32[]{:S(2)}) collective-permute-start(f32[128,256]{1,0:T(8,128)S(1)} %get-tuple-element.3), channel_id=1, source_target_pairs={{1,0},{4,1},{5,4},{8,5},{9,8},{12,9},{13,12},{0,13},{3,2},{6,3},{7... | collective-permute-start | bytes 393224 | tf_op jit(solution)/shard_map/ppermute | solution.py:19
  173.9 7.1 %copy-start.9 = (f32[256,512]{1,0:T(8,128)S(1)}, f32[256,512]{1,0:T(8,128)}, u32[]{:S(2)}) copy-start(f32[256,512]{1,0:T(8,128)} %param.50) | copy-start | bytes 1572868
  181.1 45.3 %copy-start.16 = (f32[512]{0:T(512)S(1)}, f32[512]{0:T(512)}, u32[]{:S(2)}) copy-start(f32[512]{0:T(512)} %param.51) | copy-start | bytes 6148
Sparse Core Ops, SparseCore 0:
  16.3 24.2 all-reduce.4
  64.9 21.6 all-reduce.6
  105.1 40.0 all-reduce.8
  183.2 40.2 all-reduce.10
where the time goes:
time: 236 us; the launch traced here: 235 us
  waiting for transfers between devices  125 us (53%)
  local copies, waits for them, and re-layouts  30.7 us (13%)
  other arithmetic  29.8 us (13%)
  matrix products  17.2 us (7%)
  blocking collectives  14.7 us (6%)
  between operations  14.4 us (6%)
  starting transfers between devices  3.93 us (2%)
    psum x4, waiting for transfers between devices, finish(): summed = lax.psum(partial_value, 'sub')  123 us
    dot_general x12, matrix products, project(): jnp.dot(states, weights, precision=highest, preferred_element_type=jnp.fl...  17.2 us
    gather x2, local copies, waits for them, and re-layouts, body(): picked = jnp.take(sender_rows, bottom_links, axis=0)  16.9 us
    all_gather x1, blocking collectives, body(): lax.all_gather(own_projection, ('patch', 'lvl'), axis=0, tiled=True)  14.7 us
    reduce_sum x4, other arithmetic, hidden_total(): return jnp.sum(jax.nn.silu(picked + receiver_rows[:, None, :]), axis=1)  12.4 us
    gather x2, local copies, waits for them, and re-layouts, body(): picked = jnp.take(sender_rows, down_sources, axis=0)  8.31 us
    add x4, other arithmetic, finish(): return receivers + gain_vector * layer_norm(summed)  5.93 us
    reduce_sum x4, other arithmetic, layer_norm(): spread = jnp.mean(center * center, axis=-1, keepdims=True)  5.13 us
  transfers between devices with their start and end apart: 6, of which 5 were waited for; matrix products, arithmetic and copies ran while one was open for 2% of the time, Pallas kernels for 0%

commit v1 on v0

--- a/solution.py
+++ b/solution.py
@@ -39,7 +39,8 @@
 
 def finish(receivers, hidden, output_weights, gain_vector):
     partial_value = project(hidden, output_weights)
-    summed = lax.psum(partial_value, "sub")
+    parts = lax.all_gather(partial_value, "sub")
+    summed = jnp.sum(parts, axis=0)
     return receivers + gain_vector * layer_norm(summed)
 
 

time: 236 us -> 184 us (0.78)
  waiting for transfers between devices: 125 us -> 68.7 us
  blocking collectives: 14.7 us -> 28.8 us
  matrix products: 17.2 us -> 12.9 us
  other arithmetic: 29.8 us -> 26.8 us
  local copies, waits for them, and re-layouts: 30.7 us -> 28 us
    psum x4 -> x0, waiting for transfers between devices: 123 us -> none  [finish(): summed = lax.psum(partial_value, 'sub')]
    all_gather x0 -> x2, waiting for transfers between devices: none -> 66.9 us  [finish(): parts = lax.all_gather(partial_value, 'sub')]
    all_gather x0 -> x2, blocking collectives: none -> 13.5 us  [finish(): parts = lax.all_gather(partial_value, 'sub')]
    dot_general x12, matrix products: 17.2 us -> 12.9 us  [project(): jnp.dot(states, weights, precision=highest, preferred_element_type=jnp.fl...]
    reduce_sum x4, other arithmetic: 5.13 us -> 0.87 us  [layer_norm(): spread = jnp.mean(center * center, axis=-1, keepdims=True)]
    reduce_sum x0 -> x4, other arithmetic: none -> 3.83 us  [finish(): summed = jnp.sum(parts, axis=0)]
    add x4, other arithmetic: 5.93 us -> 2.85 us  [finish(): return receivers + gain_vector * layer_norm(summed)]
    gather x2, local copies, waits for them, and re-layouts: 8.31 us -> 5.41 us  [body(): picked = jnp.take(sender_rows, down_sources, axis=0)]
  transfers between devices with their start and end apart: 6 -> 4, of which waited for: 5 -> 3; matrix products, arithmetic and copies ran while one was open for 2% -> 1% of each run, Pallas kernels for 0% -> 0%
where the time goes in v1:
time: 184 us
  waiting for transfers between devices  68.7 us (37%)
  blocking collectives  28.8 us (16%)
  local copies, waits for them, and re-layouts  28 us (15%)
  other arithmetic  26.8 us (15%)
  between operations  14.7 us (8%)
  matrix products  12.9 us (7%)
  starting transfers between devices  3.85 us (2%)
    all_gather x2, waiting for transfers between devices, finish(): parts = lax.all_gather(partial_value, 'sub')  66.9 us
    gather x2, local copies, waits for them, and re-layouts, body(): picked = jnp.take(sender_rows, bottom_links, axis=0)  16.9 us
    all_gather x1, blocking collectives, body(): lax.all_gather(own_projection, ('patch', 'lvl'), axis=0, tiled=True)  15.3 us
    all_gather x2, blocking collectives, finish(): parts = lax.all_gather(partial_value, 'sub')  13.5 us
    dot_general x12, matrix products, project(): jnp.dot(states, weights, precision=highest, preferred_element_type=jnp.fl...  12.9 us
    reduce_sum x4, other arithmetic, hidden_total(): return jnp.sum(jax.nn.silu(picked + receiver_rows[:, None, :]), axis=1)  11 us
    gather x2, local copies, waits for them, and re-layouts, body(): picked = jnp.take(sender_rows, down_sources, axis=0)  5.41 us
    reduce_sum x8, other arithmetic, layer_norm(): center = values - jnp.mean(values, axis=-1, keepdims=True)  3.91 us
  transfers between devices with their start and end apart: 4, of which 3 were waited for; matrix products, arithmetic and copies ran while one was open for 1% of the time, Pallas kernels for 0%

profile of v1, /device:TPU:0, one launch (start us, length us, event | category | flops | bytes accessed | tf_op | source)
XLA Modules:
  0.0 183.8 jit_solution(10161168155501723928)
XLA Ops:
  7.2 0.7 compare_select_fusion.3
  8.0 0.7 compare_and_fusion.4
  8.7 0.7 broadcast_clamp_fusion.1
  9.3 0.7 compare_and_fusion.3
  10.0 0.7 compare_select_fusion.1
  10.7 0.7 compare_and_fusion.1
  11.4 0.1 copy.44
  11.5 0.1 reshape.129
  11.7 2.3 %fusion.3 = f32[512,256]{1,0:T(8,128)S(1)} fusion(f32[512,512]{1,0:T(8,128)} %param.26, f32[512,256]{1,0:T(8,128)} %param.32), kind=kOutput, calls=%fused_computation.47 | convolution fusion | flops 805306368 | bytes 2097152 | tf_op jit(solution)/shard_map/dot_general | solution.py:27
  14.1 1.7 gather_fusion
  15.9 0.1 copy.43
  16.1 0.4 convolution_add_fusion.3
  16.4 0.3 multiply_reduce_fusion.4
  16.8 0.4 fusion.4
  17.3 7.1 %all-gather = f32[128,512]{1,0:T(8,128)S(1)} all-gather(f32[64,512]{1,0:T(8,128)S(1)} %fusion.4), channel_id=2, replica_groups=mesh['parts'=2,'patch'=4,'sub'=2,'lvl'=2] {'sub'}, dimensions={0}, use_global_device_ids=true | all-gather | bytes 393216 | tf_op jit(solution)/shard_map/all_gather | solution.py:42
  24.4 0.1 reduce.4
  24.5 0.1 reshape.163
  24.7 0.2 multiply_reduce_fusion.6
  24.9 0.1 multiply_add_fusion.3
  25.0 0.4 fusion.5
  25.4 15.3 %all_gather.29 = f32[512,256]{1,0:T(8,128)S(1)} all-gather(f32[64,256]{1,0:T(8,128)S(1)} %fusion.5), channel_id=1, replica_groups=mesh['parts'=2,'patch'=4,'sub'=2,'lvl'=2] {'patch','lvl'}, dimensions={0}, use_global_device_ids=true | all-gather | bytes 589824 | tf_op jit(solution)/shard_map/all_gather | solution.py:91
  40.7 0.1 copy.47
  40.8 0.1 min.12
  41.0 1.7 gather_fusion.1
  42.7 0.1 copy.45
  42.8 0.1 copy.46
  43.0 0.4 convolution_add_fusion.2
  43.4 0.5 multiply_reduce_fusion.3
  43.9 0.4 fusion.6
  44.3 6.4 %all-gather.1 = f32[128,512]{1,0:T(8,128)S(1)} all-gather(f32[64,512]{1,0:T(8,128)S(1)} %fusion.6), channel_id=3, replica_groups=mesh['parts'=2,'patch'=4,'sub'=2,'lvl'=2] {'sub'}, dimensions={0}, use_global_device_ids=true | all-gather | bytes 393216 | tf_op jit(solution)/shard_map/all_gather | solution.py:42
  50.7 0.1 reduce.6
  51.0 0.2 multiply_reduce_fusion.5
  51.2 0.2 copy.48
  51.3 0.2 reshape.145
  51.6 0.1 multiply_add_fusion.2
  51.7 0.4 fusion.7
  52.1 3.7 %gather_fusion.2 = f32[1536,256]{1,0:T(8,128)S(1)} fusion(f32[64,256]{1,0:T(8,128)S(1)} %fusion.7, s32[2048]{0:T(1024)S(1)} %pad_clamp_fusion), kind=kCustom, calls=%fused_computation.2 | custom fusion | bytes 3151872 | tf_op jit(solution)/shard_map/jit(_take)/gather | solution.py:97
  55.8 1.7 reshape.144
  57.5 0.2 copy.42
  57.7 2.2 %convolution_add_fusion.1 = f32[512,256]{1,0:T(8,128)S(1)} fusion(f32[512,512]{1,0:T(8,128)S(1)} %copy-done.1, f32[512,256]{1,0:T(8,128)} %param.43, f32[256]{0:T(256)S(1)} %copy-done.21), kind=kOutput, calls=%fused_computation.8 | convolution fusion | flops 805437440 | bytes 2098176 | tf_op jit(solution)/shard_map/dot_general | solution.py:27
  59.9 3.1 %fusion = f32[512,256]{1,0:T(8,128)S(1)} fusion(f32[512,3,256]{2,1,0:T(4,128)S(1)} %copy-done.2, f32[512,256]{1,0:T(8,128)S(1)} %convolution_add_fusion.1, pred[512,3]{1,0:T(8,128)(4,1)S(1)} %copy.42), kind=kLoop, calls=%fused_computation.6 | loop fusion | flops 2621440 | bytes 2622976 | tf_op jit(solution)/shard_map/reduce_sum | solution.py:37
  63.0 2.0 %fusion.8 = f32[512,512]{1,0:T(8,128)} fusion(f32[512,256]{1,0:T(8,128)S(1)} %fusion, f32[256,512]{1,0:T(8,128)S(1)} %copy-done), kind=kOutput, calls=%fused_computation.52 | convolution fusion | flops 805306368 | bytes 2097152 | tf_op jit(solution)/shard_map/dot_general | solution.py:27
  65.0 0.2 all-gather.9.cloned.1.call-start
  65.3 0.1 copy.50
  65.4 0.2 reshape.153
  65.6 0.2 copy.49
  65.8 33.5 %all-gather.7.cloned.1.call-done = f32[1024,512]{1,0:T(8,128)} async-done(((f32[512,512]{1,0:T(8,128)}), f32[1024,512]{1,0:T(8,128)}) %all-gather.7.cloned.1.call-update) | async-done | bytes 2097168 | tf_op jit(solution)/shard_map/all_gather | solution.py:42
  99.3 1.9 %reduce_sum.153 = f32[512,512]{1,0:T(8,128)S(1)} reduce(f32[2,512,512]{2,1,0:T(8,128)} %bitcast.28, f32[]{:T(128)} %constant.80.clone.1), dimensions={0}, to_apply=%region_9.10 | reduce | flops 262144 | bytes 3145732 | tf_op jit(solution)/shard_map/reduce_sum | solution.py:43
  101.2 1.8 reduce.8
  103.1 0.3 multiply_reduce_fusion.2
  103.4 1.5 multiply_add_fusion.1
  104.9 1.0 fusion.9
  106.0 3.5 %collective-permute-start.1 = (f32[128,256]{1,0:T(8,128)S(1)}, f32[128,256]{1,0:T(8,128)S(1)}, u32[]{:S(2)}, u32[]{:S(2)}) collective-permute-start(f32[128,256]{1,0:T(8,128)S(1)} %get-tuple-element.3), channel_id=1, source_target_pairs={{1,0},{4,1},{5,4},{8,5},{9,8},{12,9},{13,12},{0,13},{3,2},{6,3},{7... | collective-permute-start | bytes 393224 | tf_op jit(solution)/shard_map/ppermute | solution.py:19
  109.5 1.0 convolution_add_fusion
  110.5 1.7 collective-permute-done
  112.3 12.3 %gather_fusion.3 = f32[3072,256]{1,0:T(8,128)} fusion(f32[768,256]{1,0:T(8,128)S(1)} %pad_maximum_fusion, s32[3072]{0:T(1024)S(1)} %broadcast_clamp_fusion), kind=kCustom, calls=%fused_computation.3 | custom fusion | bytes 6303744 | tf_op jit(solution)/shard_map/jit(_take)/gather | solution.py:105
  124.6 4.5 %reshape.152 = f32[512,6,256]{2,1,0:T(8,128)} reshape(f32[3072,256]{1,0:T(8,128)} %gather_fusion.3) | data formatting | bytes 6291456 | tf_op jit(solution)/shard_map/jit(_take)/gather | solution.py:105
  129.2 7.1 %multiply_reduce_fusion = f32[512,256]{1,0:T(8,128)S(1)} fusion(f32[512,6,256]{2,1,0:T(8,128)} %reshape.152, f32[512,256]{1,0:T(8,128)S(1)} %convolution_add_fusion, pred[512,6]{1,0:T(8,128)(4,1)S(1)} %copy.49), kind=kLoop, calls=%fused_computation.4 | loop fusion | flops 5373952 | bytes 4197376 | tf_op jit(solution)/shard_map/reduce_sum | solution.py:37
  136.3 2.0 %fusion.10 = f32[512,512]{1,0:T(8,128)} fusion(f32[512,256]{1,0:T(8,128)S(1)} %multiply_reduce_fusion, f32[256,512]{1,0:T(8,128)S(1)} %copy-done.13), kind=kOutput, calls=%fused_computation.54 | convolution fusion | flops 805306368 | bytes 2097152 | tf_op jit(solution)/shard_map/dot_general | solution.py:27
  138.3 33.4 %all-gather.9.cloned.1.call-done = f32[1024,512]{1,0:T(8,128)} async-done(((f32[512,512]{1,0:T(8,128)}), f32[1024,512]{1,0:T(8,128)}) %all-gather.9.cloned.1.call-update) | async-done | bytes 2097168 | tf_op jit(solution)/shard_map/all_gather | solution.py:42
  171.7 1.9 %reduce_sum.157 = f32[512,512]{1,0:T(8,128)S(1)} reduce(f32[2,512,512]{2,1,0:T(8,128)} %bitcast.29, f32[]{:T(128)} %constant.80.clone.1), dimensions={0}, to_apply=%region_13.14 | reduce | flops 262144 | bytes 3145732 | tf_op jit(solution)/shard_map/reduce_sum | solution.py:43
  173.6 1.8 reduce.10
  175.5 0.3 multiply_reduce_fusion.1
  175.7 1.2 multiply_add_fusion
  (79 shorter events, 0.9 us)
Async XLA Ops:
  7.2 55.8 %copy-start = (f32[256,512]{1,0:T(8,128)S(1)}, f32[256,512]{1,0:T(8,128)}, u32[]{:S(2)}) copy-start(f32[256,512]{1,0:T(8,128)} %param.45) | copy-start | bytes 1572868
  7.2 92.2 %all-gather.7.cloned.1.call-start = ((), (), s32[]{:S(2)}) async-start(), calls=%async_computation | async-start | bytes 3145728 | tf_op jit(solution)/shard_map/all_gather | solution.py:42
  14.0 2.0 %copy-start.3 = (f32[512,256]{1,0:T(8,128)S(1)}, f32[512,256]{1,0:T(8,128)}, u32[]{:S(2)}) copy-start(f32[512,256]{1,0:T(8,128)} %param.33) | copy-start | bytes 1572868
  14.1 2.0 %copy-start.9 = (f32[64,512]{1,0:T(8,128)S(1)}, f32[64,512]{1,0:T(8,128)}, u32[]{:S(2)}) copy-start(f32[64,512]{1,0:T(8,128)} %param.27) | copy-start | bytes 393220
  14.1 2.0 %copy-start.19 = (f32[256]{0:T(256)S(1)}, f32[256]{0:T(256)}, u32[]{:S(2)}) copy-start(f32[256]{0:T(256)} %param.34) | copy-start | bytes 3076
  15.8 1.0 copy-start.4
  15.8 9.0 %copy-start.15 = (f32[512]{0:T(512)S(1)}, f32[512]{0:T(512)}, u32[]{:S(2)}) copy-start(f32[512]{0:T(512)} %param.36) | copy-start | bytes 6148
  15.9 9.1 %copy-start.5 = (f32[512,256]{1,0:T(8,128)S(1)}, f32[512,256]{1,0:T(8,128)}, u32[]{:S(2)}) copy-start(f32[512,256]{1,0:T(8,128)} %param.37) | copy-start | bytes 1572868
  40.9 2.0 %copy-start.6 = (f32[512,256]{1,0:T(8,128)S(1)}, f32[512,256]{1,0:T(8,128)}, u32[]{:S(2)}) copy-start(f32[512,256]{1,0:T(8,128)} %param.38) | copy-start | bytes 1572868
  40.9 2.0 %copy-start.20 = (f32[256]{0:T(256)S(1)}, f32[256]{0:T(256)}, u32[]{:S(2)}) copy-start(f32[256]{0:T(256)} %param.39) | copy-start | bytes 3076
  41.0 2.9 %copy-start.7 = (f32[256,512]{1,0:T(8,128)S(1)}, f32[256,512]{1,0:T(8,128)}, u32[]{:S(2)}) copy-start(f32[256,512]{1,0:T(8,128)} %param.40) | copy-start | bytes 1572868
  42.7 8.8 %copy-start.16 = (f32[512]{0:T(512)S(1)}, f32[512]{0:T(512)}, u32[]{:S(2)}) copy-start(f32[512]{0:T(512)} %param.41) | copy-start | bytes 6148
  43.0 8.7 %copy-start.8 = (f32[512,256]{1,0:T(8,128)S(1)}, f32[512,256]{1,0:T(8,128)}, u32[]{:S(2)}) copy-start(f32[512,256]{1,0:T(8,128)} %param.42) | copy-start | bytes 1572868
  51.7 4.1 %copy-start.10 = (f32[64,512]{1,0:T(8,128)}, f32[64,512]{1,0:T(8,128)S(1)}, u32[]{:S(2)}) copy-start(f32[64,512]{1,0:T(8,128)S(1)} %multiply_add_fusion.2) | copy-start | bytes 393220
  55.8 2.0 %copy-start.1 = (f32[512,512]{1,0:T(8,128)S(1)}, f32[512,512]{1,0:T(8,128)}, u32[]{:S(2)}) copy-start(f32[512,512]{1,0:T(8,128)} %param.26) | copy-start | bytes 3145732
  55.8 2.0 %copy-start.21 = (f32[256]{0:T(256)S(1)}, f32[256]{0:T(256)}, u32[]{:S(2)}) copy-start(f32[256]{0:T(256)} %param.44) | copy-start | bytes 3076
  57.7 2.2 %copy-start.2 = (f32[512,3,256]{2,1,0:T(4,128)S(1)}, f32[512,3,256]{2,1,0:T(4,128)}, u32[]{:S(2)}) copy-start(f32[512,3,256]{2,1,0:T(4,128)} %reshape.144) | copy-start | bytes 4718596
  63.0 2.3 %copy-start.14 = (s32[512,6]{0,1:T(8,128)S(1)}, s32[512,6]{0,1:T(8,128)}, u32[]{:S(2)}) copy-start(s32[512,6]{0,1:T(8,128)} %param.30) | copy-start | bytes 36868
  65.0 106.7 %all-gather.9.cloned.1.call-start = ((), (), s32[]{:S(2)}) async-start(), calls=%async_computation.1 | async-start | bytes 3145728 | tf_op jit(solution)/shard_map/all_gather | solution.py:42
  101.2 2.1 %copy-start.17 = (f32[512]{0:T(512)S(1)}, f32[512]{0:T(512)}, u32[]{:S(2)}) copy-start(f32[512]{0:T(512)} %param.46) | copy-start | bytes 6148
  103.1 1.8 copy-start.11
  104.9 4.6 %copy-start.12 = (f32[512,256]{1,0:T(8,128)S(1)}, f32[512,256]{1,0:T(8,128)}, u32[]{:S(2)}) copy-start(f32[512,256]{1,0:T(8,128)} %param.48) | copy-start | bytes 1572868
  104.9 4.6 %copy-start.22 = (f32[256]{0:T(256)S(1)}, f32[256]{0:T(256)}, u32[]{:S(2)}) copy-start(f32[256]{0:T(256)} %param.49) | copy-start | bytes 3076
  105.9 6.3 %collective-permute-start = (f32[128,256]{1,0:T(8,128)S(1)}, f32[128,256]{1,0:T(8,128)S(1)}, u32[]{:S(2)}, u32[]{:S(2)}) collective-permute-start(f32[128,256]{1,0:T(8,128)S(1)} %get-tuple-element.2), channel_id=1, source_target_pairs={{0,1},{1,4},{4,5},{5,8},{8,9},{9,12},{12,13},{13,0},{2,3},{3,6},{6... | collective-permute-start | bytes 393224 | tf_op jit(solution)/shard_map/ppermute | solution.py:17
  106.0 6.3 %collective-permute-start.1 = (f32[128,256]{1,0:T(8,128)S(1)}, f32[128,256]{1,0:T(8,128)S(1)}, u32[]{:S(2)}, u32[]{:S(2)}) collective-permute-start(f32[128,256]{1,0:T(8,128)S(1)} %get-tuple-element.3), channel_id=1, source_target_pairs={{1,0},{4,1},{5,4},{8,5},{9,8},{12,9},{13,12},{0,13},{3,2},{6,3},{7... | collective-permute-start | bytes 393224 | tf_op jit(solution)/shard_map/ppermute | solution.py:19
  129.2 7.1 %copy-start.13 = (f32[256,512]{1,0:T(8,128)S(1)}, f32[256,512]{1,0:T(8,128)}, u32[]{:S(2)}) copy-start(f32[256,512]{1,0:T(8,128)} %param.50) | copy-start | bytes 1572868
  173.6 2.1 %copy-start.18 = (f32[512]{0:T(512)S(1)}, f32[512]{0:T(512)}, u32[]{:S(2)}) copy-start(f32[512]{0:T(512)} %param.51) | copy-start | bytes 6148
Sparse Core Ops, SparseCore 0:
  65.2 34.1 all-gather.6
  138.4 33.2 all-gather.8
